TPU v7x, 768 devices: a whole 4x8x12 slice. The times are simulated.
768 devices in a mesh: dp: 12 (over z), tensor: 64 (over x, y, core).
Axes of the slice: x: 4, y: 8, z: 12, core: 2. Of those that a mesh axis runs over, the one named last changes fastest.
Arguments:
- tokens: bfloat16 [1536, 2048], P(('dp', 'tensor')), may hold values from -6 to 6
- cotangent: bfloat16 [1536, 2048], P(('dp', 'tensor')), may hold values from -6 to 6
- levels: int32 [12], replicated, may hold values from 0 to 3, as said below
- gate_weight: bfloat16 [2048, 16384], P(None, 'tensor'), may hold values from -0.125 to 0.125
- up_weight: bfloat16 [2048, 16384], P(None, 'tensor'), may hold values from -0.125 to 0.125
- down_weight: bfloat16 [16384, 2048], P('tensor'), may hold values from -0.046875 to 0.046875
Outputs:
- mixed: bfloat16 [1536, 2048], P(('dp', 'tensor'))
- input_grad: bfloat16 [1536, 2048], P(('dp', 'tensor'))
- gate_grad: bfloat16 [2048, 16384], P(None, 'tensor')
- up_grad: bfloat16 [2048, 16384], P(None, 'tensor')
- down_grad: bfloat16 [16384, 2048], P('tensor')
Inputs may be any that keep to these rules, and one draw needn't show every extreme that they name: `levels`: every level from 0 to 3 is taken by at least one group in every draw.
All inputs are finite; a program needn't handle non-finite values.
Results may differ from a plain program's by a relative error of at most 0.014.
Values may be sent and summed in bfloat16 or wider, within the bound.
A program may use at most 128 MiB of HBM per device.

v0:
```python
import jax
import jax.numpy as jnp
from jax import lax
from jax.sharding import PartitionSpec as P

FF = 16384


def in_order(parts, dim):
    dims = list(parts.shape[1:])
    dims[dim] *= parts.shape[0]
    return jnp.moveaxis(parts, 0, dim).reshape(dims)


def from_everyone(value, axis):
    copies = jnp.broadcast_to(value, (lax.axis_size(axis), *value.shape))
    return lax.all_to_all(copies, axis, split_axis=0, concat_axis=0, tiled=True)


def gather_directly(value, axis, dim):
    return in_order(from_everyone(value, axis), dim)


def cut_along(value, dim, length):
    before, after = (value.shape[:dim], value.shape[dim + 1 :])
    return jnp.moveaxis(value.reshape(*before, length, -1, *after), dim, 0)


def sum_at_owner(value, axis, dim):
    length = lax.axis_size(axis)
    parts = lax.all_to_all(cut_along(value, dim, length), axis, 0, 0, tiled=True)
    return jnp.sum(parts, axis=0)


def body(tokens, cotangent, levels, gate_weight, up_weight, down_weight):
    local_units = gate_weight.shape[1]
    group_index = lax.axis_index("dp")
    tensor_index = lax.axis_index("tensor")
    level_now = levels[group_index]
    prefix_width = jnp.right_shift(jnp.int32(FF), level_now)
    unit_index = tensor_index * local_units + lax.iota(jnp.int32, local_units)
    active_mask = (unit_index < prefix_width)[None, :]
    group_rows = gather_directly(tokens, "tensor", 0)
    group_cot = gather_directly(cotangent, "tensor", 0)
    gate_value = jnp.dot(group_rows, gate_weight, preferred_element_type=jnp.float32)
    up_value = jnp.dot(group_rows, up_weight, preferred_element_type=jnp.float32)
    sigmoid_gate = 1.0 / (1.0 + jnp.exp(-gate_value))
    hidden = jnp.where(active_mask, gate_value * sigmoid_gate * up_value, 0.0).astype(jnp.bfloat16)
    mixed = sum_at_owner(
        jnp.dot(hidden, down_weight, preferred_element_type=jnp.float32), "tensor", 0
    ).astype(jnp.bfloat16)
    hidden_grad = jnp.dot(group_cot, down_weight.T, preferred_element_type=jnp.float32)
    hidden_grad = jnp.where(active_mask, hidden_grad, 0.0)
    gate_act = (
        hidden_grad * up_value * sigmoid_gate * (1.0 + gate_value * (1.0 - sigmoid_gate))
    ).astype(jnp.bfloat16)
    up_act = (hidden_grad * gate_value * sigmoid_gate).astype(jnp.bfloat16)
    input_grad = sum_at_owner(
        jnp.dot(gate_act, gate_weight.T, preferred_element_type=jnp.float32)
        + jnp.dot(up_act, up_weight.T, preferred_element_type=jnp.float32),
        "tensor",
        0,
    ).astype(jnp.bfloat16)
    model_width = group_rows.shape[1]
    gate_partial = jnp.dot(group_rows.T, gate_act, preferred_element_type=jnp.float32)
    up_partial = jnp.dot(group_rows.T, up_act, preferred_element_type=jnp.float32)
    down_partial_t = jnp.dot(group_cot.T, hidden, preferred_element_type=jnp.float32)
    stacked = jnp.concatenate([gate_partial, up_partial, down_partial_t], axis=0)
    shares = lax.psum_scatter(stacked.astype(jnp.bfloat16), "dp", scatter_dimension=0, tiled=True)
    summed = lax.all_gather(shares, "dp", axis=0, tiled=True)
    gate_out = summed[:model_width]
    up_out = summed[model_width : 2 * model_width]
    down_out = summed[2 * model_width :].T
    return (mixed, input_grad, gate_out, up_out, down_out)


def solution(mesh):
    in_specs = (
        P(("dp", "tensor"), None),
        P(("dp", "tensor"), None),
        P(),
        P(None, "tensor"),
        P(None, "tensor"),
        P("tensor", None),
    )
    out_specs = (
        P(("dp", "tensor"), None),
        P(("dp", "tensor"), None),
        P(None, "tensor"),
        P(None, "tensor"),
        P("tensor", None),
    )
    return jax.shard_map(body, mesh=mesh, in_specs=in_specs, out_specs=out_specs, check_vma=False)
```

profile of v0, /device:TPU:1, one launch (start us, length us, event | category | flops | bytes accessed | tf_op | source)
XLA Modules:
  0.0 225.6 jit_solution(10153153388283237661)
XLA Ops:
  7.2 1.1 broadcast_in_dim.24
  8.3 31.1 %all_to_all.20 = bf16[64,2,2048]{2,1,0:T(2,128)(2,1)S(1)} all-to-all(bf16[64,2,2048]{2,1,0:T(2,128)(2,1)S(1)} %broadcast_in_dim.24), channel_id=1, replica_groups=mesh['dp'=12,'tensor'=64] {'tensor'}, dimensions={0} | all-to-all | bytes 1048576 | tf_op jit(solution)/shard_map/all_to_all | solution.py:17
  39.4 1.8 broadcast_in_dim.26
  41.1 6.5 %all-to-all-start.2 = ((bf16[64,2,2048]{2,1,0:T(2,128)(2,1)}), bf16[64,2,2048]{2,1,0:T(2,128)(2,1)}, u32[]{:S(2)}, u32[]{:S(2)}) async-start(bf16[64,2,2048]{2,1,0:T(2,128)(2,1)} %broadcast_in_dim.26), calls=%async_computation.2 | async-start | bytes 1048576 | tf_op jit(solution)/shard_map/all_to_all | solution.py:17
  47.7 0.0 reduce-scatter.2.cloned.1.call-start
  47.8 0.6 dynamic_slice.3
  49.0 0.2 reshape.29
  49.2 1.5 fusion.3
  50.8 1.0 fusion.4
  51.7 13.1 %all-to-all-done.2 = bf16[64,2,2048]{2,1,0:T(2,128)(2,1)} async-done(((bf16[64,2,2048]{2,1,0:T(2,128)(2,1)}), bf16[64,2,2048]{2,1,0:T(2,128)(2,1)}, u32[]{:S(2)}, u32[]{:S(2)}) %all-to-all-start.2) | async-done | bytes 524320 | tf_op jit(solution)/shard_map/all_to_all | solution.py:17
  64.9 1.2 reshape.31
  66.1 1.4 multiply_convert_fusion
  67.6 0.4 fusion.2
  68.0 0.4 fusion.1
  68.5 0.4 fusion
  68.9 1.8 pad_maximum_fusion
  70.7 0.0 all-gather.2.cloned.1.call-start
  70.8 58.2 %reduce-scatter.2.cloned.1.call-done = bf16[512,256]{0,1:T(8,128)(2,1)} async-done(((bf16[6144,256]{0,1:T(8,128)(2,1)}), bf16[512,256]{0,1:T(8,128)(2,1)}) %reduce-scatter.2.cloned.1.call-update) | async-done | bytes 262160 | tf_op jit(solution)/shard_map/reduce_scatter | solution.py:69
  129.0 0.3 fusion.5
  129.3 1.6 reshape.30
  130.9 18.0 %all-to-all-start.1 = ((f32[64,2,2048]{2,1,0:T(2,128)}), f32[64,2,2048]{2,1,0:T(2,128)}, u32[]{:S(2)}, u32[]{:S(2)}) async-start(f32[64,2,2048]{2,1,0:T(2,128)} %reshape.30), calls=%async_computation.1 | async-start | bytes 2097152 | tf_op jit(solution)/shard_map/all_to_all | solution.py:31
  148.9 1.7 fusion.6
  150.6 0.5 convolution_add_fusion
  151.1 1.6 reshape.32
  152.7 24.7 %all-to-all-done.1 = f32[64,2,2048]{2,1,0:T(2,128)} async-done(((f32[64,2,2048]{2,1,0:T(2,128)}), f32[64,2,2048]{2,1,0:T(2,128)}, u32[]{:S(2)}, u32[]{:S(2)}) %all-to-all-start.1) | async-done | bytes 1048608 | tf_op jit(solution)/shard_map/all_to_all | solution.py:31
  177.3 6.2 %all-to-all-start.3 = ((f32[64,2,2048]{2,1,0:T(2,128)}), f32[64,2,2048]{2,1,0:T(2,128)S(1)}, u32[]{:S(2)}, u32[]{:S(2)}) async-start(f32[64,2,2048]{2,1,0:T(2,128)} %reshape.32), calls=%async_computation.3 | async-start | bytes 2097152 | tf_op jit(solution)/shard_map/all_to_all | solution.py:31
  183.5 2.2 reduce_sum.18
  185.7 26.4 %all-to-all-done.3 = f32[64,2,2048]{2,1,0:T(2,128)S(1)} async-done(((f32[64,2,2048]{2,1,0:T(2,128)}), f32[64,2,2048]{2,1,0:T(2,128)S(1)}, u32[]{:S(2)}, u32[]{:S(2)}) %all-to-all-start.3) | async-done | bytes 1048608 | tf_op jit(solution)/shard_map/all_to_all | solution.py:31
  212.1 1.0 reduce_sum.19
  213.0 3.1 %slice_bitcast_fusion = (bf16[256,2048]{1,0:T(8,128)(2,1)}, bf16[2048,256]{0,1:T(8,128)(2,1)S(1)}, bf16[2048,256]{0,1:T(8,128)(2,1)S(1)}) fusion(bf16[6144,256]{0,1:T(8,128)(2,1)} %all-gather.2.cloned.1.call-done), kind=kLoop, calls=%fused_computation.9 | loop fusion | bytes 6291456 | tf_op jit(solution)/shard_map/transpose | solution.py:73
  216.2 1.3 copy.11
  217.5 1.3 copy.12
  (10 shorter events, 0.1 us)
Async XLA Ops:
  7.2 59.0 %copy-start = (bf16[256,2048]{1,0:T(8,128)(2,1)S(1)}, bf16[256,2048]{1,0:T(8,128)(2,1)}, u32[]{:S(2)}) copy-start(bf16[256,2048]{1,0:T(8,128)(2,1)} %param.11) | copy-start | bytes 3145732
  7.2 40.6 %copy-start.2 = (s32[12]{0:T(128)S(1)}, s32[12]{0:T(128)}, u32[]{:S(2)}) copy-start(s32[12]{0:T(128)} %param.8) | copy-start | bytes 148
  7.2 43.6 %copy-start.1 = (bf16[2048,256]{1,0:T(8,128)(2,1)S(1)}, bf16[2048,256]{1,0:T(8,128)(2,1)}, u32[]{:S(2)}) copy-start(bf16[2048,256]{1,0:T(8,128)(2,1)} %param.10) | copy-start | bytes 3145732
  41.1 23.8 %all-to-all-start.2 = ((bf16[64,2,2048]{2,1,0:T(2,128)(2,1)}), bf16[64,2,2048]{2,1,0:T(2,128)(2,1)}, u32[]{:S(2)}, u32[]{:S(2)}) async-start(bf16[64,2,2048]{2,1,0:T(2,128)(2,1)} %broadcast_in_dim.26), calls=%async_computation.2 | async-start | bytes 1048576 | tf_op jit(solution)/shard_map/all_to_all | solution.py:17
  47.7 81.3 %reduce-scatter.2.cloned.1.call-start = ((), (), s32[]{:S(2)}) async-start(), calls=%async_computation.5 | async-start | bytes 3407872 | tf_op jit(solution)/shard_map/reduce_scatter | solution.py:69
  70.7 142.3 %all-gather.2.cloned.1.call-start = ((), (), s32[]{:S(2)}) async-start(), calls=%async_computation.6 | async-start | bytes 3407872 | tf_op jit(solution)/shard_map/all_gather | solution.py:70
  130.9 46.4 %all-to-all-start.1 = ((f32[64,2,2048]{2,1,0:T(2,128)}), f32[64,2,2048]{2,1,0:T(2,128)}, u32[]{:S(2)}, u32[]{:S(2)}) async-start(f32[64,2,2048]{2,1,0:T(2,128)} %reshape.30), calls=%async_computation.1 | async-start | bytes 2097152 | tf_op jit(solution)/shard_map/all_to_all | solution.py:31
  177.3 34.7 %all-to-all-start.3 = ((f32[64,2,2048]{2,1,0:T(2,128)}), f32[64,2,2048]{2,1,0:T(2,128)S(1)}, u32[]{:S(2)}, u32[]{:S(2)}) async-start(f32[64,2,2048]{2,1,0:T(2,128)} %reshape.32), calls=%async_computation.3 | async-start | bytes 2097152 | tf_op jit(solution)/shard_map/all_to_all | solution.py:31
Sparse Core Ops, SparseCore 0:
  70.8 58.0 reduce-scatter.1
  131.4 62.2 all-gather.1
where the time goes:
time: 226 us
  waiting for transfers between devices  122 us (54%)
  blocking collectives  31.1 us (14%)
  starting transfers between devices  30.8 us (14%)
  between operations  14.9 us (7%)
  local copies, waits for them, and re-layouts  13.8 us (6%)
  matrix products  7.74 us (3%)
  other arithmetic  4.91 us (2%)
    reduce_scatter x1, waiting for transfers between devices, body(): lax.psum_scatter(stacked.astype(jnp.bfloat16), 'dp', scatter_dimension=0,...  58.2 us
    all_to_all x2, waiting for transfers between devices, sum_at_owner(): lax.all_to_all(cut_along(value, dim, length), axis, 0, 0, tiled=True)  51 us
    all_to_all x1, blocking collectives, from_everyone(): return lax.all_to_all(copies, axis, split_axis=0, concat_axis=0, tiled=True)  31.1 us
    all_to_all x2, starting transfers between devices, sum_at_owner(): lax.all_to_all(cut_along(value, dim, length), axis, 0, 0, tiled=True)  24.2 us
    all_to_all x1, waiting for transfers between devices, from_everyone(): return lax.all_to_all(copies, axis, split_axis=0, concat_axis=0, tiled=True)  13.1 us
    all_to_all x1, starting transfers between devices, from_everyone(): return lax.all_to_all(copies, axis, split_axis=0, concat_axis=0, tiled=True)  6.55 us
  transfers between devices with their start and end apart: 5, of which 4 were waited for; matrix products, arithmetic and copies ran while one was open for 5% of the time, Pallas kernels for 0%

commit v1 on v0

v1 whole, which is shorter than its diff:
```python
import jax
import jax.numpy as jnp
from jax import lax
from jax.sharding import PartitionSpec as P

FF = 16384
GROUPS = 12
TOK_GROUP = 128


def body(tokens, cotangent, levels, gate_weight, up_weight, down_weight):
    local_units = gate_weight.shape[1]
    group_index = lax.axis_index("dp")
    tensor_index = lax.axis_index("tensor")
    all_tokens = lax.all_gather(tokens, ("dp", "tensor"), axis=0, tiled=True)
    all_cot = lax.all_gather(cotangent, ("dp", "tensor"), axis=0, tiled=True)
    prefix = jnp.right_shift(jnp.int32(FF), levels)
    unit_index = tensor_index * local_units + lax.iota(jnp.int32, local_units)
    active = (unit_index[None, :] < prefix[:, None])
    active = jnp.repeat(active, TOK_GROUP, axis=0)
    gate_value = jnp.dot(all_tokens, gate_weight, preferred_element_type=jnp.float32)
    up_value = jnp.dot(all_tokens, up_weight, preferred_element_type=jnp.float32)
    sigmoid_gate = 1.0 / (1.0 + jnp.exp(-gate_value))
    hidden = jnp.where(active, gate_value * sigmoid_gate * up_value, 0.0).astype(jnp.bfloat16)
    hidden_grad = jnp.dot(all_cot, down_weight.T, preferred_element_type=jnp.float32)
    hidden_grad = jnp.where(active, hidden_grad, 0.0)
    gate_act = (
        hidden_grad * up_value * sigmoid_gate * (1.0 + gate_value * (1.0 - sigmoid_gate))
    ).astype(jnp.bfloat16)
    up_act = (hidden_grad * gate_value * sigmoid_gate).astype(jnp.bfloat16)

    def mine(value):
        return lax.dynamic_slice_in_dim(value, group_index * TOK_GROUP, TOK_GROUP, 0)

    mixed = jnp.dot(mine(hidden), down_weight, preferred_element_type=jnp.float32)
    input_grad = jnp.dot(mine(gate_act), gate_weight.T, preferred_element_type=jnp.float32) + jnp.dot(
        mine(up_act), up_weight.T, preferred_element_type=jnp.float32
    )
    both = jnp.concatenate([mixed.astype(jnp.bfloat16), input_grad.astype(jnp.bfloat16)], axis=1)
    both = lax.psum_scatter(both, "tensor", scatter_dimension=0, tiled=True)
    width = mixed.shape[1]
    gate_out = jnp.dot(all_tokens.T, gate_act, preferred_element_type=jnp.float32).astype(jnp.bfloat16)
    up_out = jnp.dot(all_tokens.T, up_act, preferred_element_type=jnp.float32).astype(jnp.bfloat16)
    down_out = jnp.dot(hidden.T, all_cot, preferred_element_type=jnp.float32).astype(jnp.bfloat16)
    return (both[:, :width], both[:, width:], gate_out, up_out, down_out)


def solution(mesh):
    rows = P(("dp", "tensor"), None)
    columns = P(None, "tensor")
    units = P("tensor", None)
    return jax.shard_map(
        body,
        mesh=mesh,
        in_specs=(rows, rows, P(), columns, columns, units),
        out_specs=(rows, rows, columns, columns, units),
        check_vma=False,
    )
```

time: 226 us -> 614 us (2.72)
  waiting for transfers between devices: 122 us -> 540 us
  blocking collectives: 31.1 us -> 0 us
  starting transfers between devices: 30.8 us -> 0.11 us
  matrix products: 7.74 us -> 27.6 us
  local copies, waits for them, and re-layouts: 13.8 us -> 27.9 us
    all_gather x1 -> x2, waiting for transfers between devices: 0.01 us -> 341 us  [the longest x1 183 us: body(): all_tokens = lax.all_gather(tokens, ('dp', 'tensor'), axis=0, tiled=True)]
    unnamed x2 -> x4, waiting for transfers between devices: 0.03 us -> 199 us
    all_to_all x3 -> x0, waiting for transfers between devices: 64.2 us -> none  [the longest x2 51 us: sum_at_owner(): lax.all_to_all(cut_along(value, dim, length), axis, 0, 0, tiled=True)]
    reduce_scatter x1 -> x0, waiting for transfers between devices: 58.2 us -> none  [body(): lax.psum_scatter(stacked.astype(jnp.bfloat16), 'dp', scatter_dimension=0,...]
    all_to_all x1 -> x0, blocking collectives: 31.1 us -> none  [from_everyone(): return lax.all_to_all(copies, axis, split_axis=0, concat_axis=0, tiled=True)]
    all_to_all x3 -> x0, starting transfers between devices: 30.7 us -> none  [the longest x2 24.2 us: sum_at_owner(): lax.all_to_all(cut_along(value, dim, length), axis, 0, 0, tiled=True)]
    unnamed x8 -> x21, local copies, waits for them, and re-layouts: 2.62 us -> 26.3 us
    dot_general x9, matrix products: 7.74 us -> 27.6 us  [the longest x1 5.74 us: body(): jnp.dot(all_tokens, gate_weight, preferred_element_type=jnp.float32)]
  transfers between devices with their start and end apart: 5 -> 3, of which waited for: 4 -> 3; matrix products, arithmetic and copies ran while one was open for 5% -> 4% of each run, Pallas kernels for 0% -> 0%
where the time goes in v1:
time: 614 us; the launch traced here: 612 us
  waiting for transfers between devices  540 us (88%)
  local copies, waits for them, and re-layouts  27.9 us (5%)
  matrix products  27.6 us (4%)
  between operations  14.5 us (2%)
    unnamed x4, waiting for transfers between devices  199 us
    all_gather x1, waiting for transfers between devices, body(): all_tokens = lax.all_gather(tokens, ('dp', 'tensor'), axis=0, tiled=True)  183 us
    all_gather x1, waiting for transfers between devices, body(): all_cot = lax.all_gather(cotangent, ('dp', 'tensor'), axis=0, tiled=True)  159 us
    unnamed x21, local copies, waits for them, and re-layouts  26.3 us
  transfers between devices with their start and end apart: 3, of which 3 were waited for; matrix products, arithmetic and copies ran while one was open for 4% of the time, Pallas kernels for 0%

profile of v1, /device:TPU:1, one launch (start us, length us, event | category | flops | bytes accessed | tf_op | source)
XLA Modules:
  0.0 612.4 jit_solution(6206227854612577407)
XLA Ops:
  7.2 0.0 copy-start
  7.2 0.0 all-gather.5.cloned.1.call-start
  7.2 0.7 all-gather.5.cloned.1.call-update
  7.9 0.0 all-gather.7.cloned.1.call-start
  8.0 0.7 all-gather.7.cloned.1.call-update
  8.7 0.0 all-reduce.3.cloned.1.call-start
  8.7 1.3 dynamic-slice
  10.7 0.7 broadcast_shift-right-arithmetic_fusion
  11.3 0.1 broadcast_compare_fusion
  11.4 182.8 %all-gather.5.cloned.1.call-done = bf16[768,2,2048]{2,1,0:T(2,128)(2,1)} async-done(((bf16[1,2,2048]{2,1,0:T(2,128)(2,1)}), bf16[768,2,2048]{2,1,0:T(2,128)(2,1)}) %all-gather.5.cloned.1.call-update) | async-done | bytes 6291472 | tf_op jit(solution)/shard_map/all_gather | solution.py:15
  194.2 10.2 %reshape.20 = bf16[1536,2048]{1,0:T(8,128)(2,1)} reshape(bf16[768,2,2048]{2,1,0:T(2,128)(2,1)} %all-gather.5.cloned.1.call-done) | data formatting | bytes 12582912
  204.4 5.7 fusion.12
  210.1 158.5 %all-gather.7.cloned.1.call-done = bf16[768,2,2048]{2,1,0:T(2,128)(2,1)} async-done(((bf16[1,2,2048]{2,1,0:T(2,128)(2,1)}), bf16[768,2,2048]{2,1,0:T(2,128)(2,1)}) %all-gather.7.cloned.1.call-update) | async-done | bytes 6291472 | tf_op jit(solution)/shard_map/all_gather | solution.py:16
  368.6 10.2 %reshape.22 = bf16[1536,2048]{1,0:T(8,128)(2,1)} reshape(bf16[768,2,2048]{2,1,0:T(2,128)(2,1)} %all-gather.7.cloned.1.call-done) | data formatting | bytes 12582912
  378.8 0.1 broadcast_in_dim.10
  378.9 0.0 slice-start.1
  378.9 4.8 convolution_select_fusion
  383.8 0.2 copy-done.1
  383.9 2.5 fusion.3
  386.4 0.0 copy-start.3
  386.4 2.8 fusion
  389.2 1.4 fusion.5
  390.7 0.3 convolution_convert_fusion.3
  391.0 2.8 fusion.1
  393.8 2.3 copy.14
  396.0 2.3 copy.13
  398.3 1.7 fusion.2
  400.0 1.1 pad_maximum_fusion
  401.1 0.0 all-reduce.3.cloned.1.call-update
  401.1 5.6 convolution_convert_fusion
  406.7 197.7 %all-reduce.3.cloned.1.call-done = bf16[128,4096]{1,0:T(8,128)(2,1)} async-done(((bf16[128,4096]{1,0:T(8,128)(2,1)}), bf16[128,4096]{1,0:T(8,128)(2,1)}) %all-reduce.3.cloned.1.call-update) | async-done | bytes 1048592
  604.4 1.5 fusion.11
  (14 shorter events, 0.0 us)
Async XLA Ops:
  7.2 376.6 %copy-start = (bf16[2048,256]{1,0:T(8,128)(2,1)S(1)}, bf16[2048,256]{1,0:T(8,128)(2,1)}, u32[]{:S(2)}) copy-start(bf16[2048,256]{1,0:T(8,128)(2,1)} %param.10) | copy-start | bytes 3145732
  7.2 187.0 %all-gather.5.cloned.1.call-start = ((), (), s32[]{:S(2)}) async-start(), calls=%async_computation | async-start | bytes 6299648 | tf_op jit(solution)/shard_map/all_gather | solution.py:15
  7.9 360.7 %all-gather.7.cloned.1.call-start = ((), (), s32[]{:S(2)}) async-start(), calls=%async_computation.1 | async-start | bytes 6299648 | tf_op jit(solution)/shard_map/all_gather | solution.py:16
  8.7 595.7 %all-reduce.3.cloned.1.call-start = ((), (), s32[]{:S(2)}) async-start(), calls=%async_computation.2 | async-start | bytes 2097152
  11.4 193.0 %copy-start.2 = (bf16[2048,256]{1,0:T(8,128)(2,1)S(1)}, bf16[2048,256]{1,0:T(8,128)(2,1)}, u32[]{:S(2)}) copy-start(bf16[2048,256]{1,0:T(8,128)(2,1)} %param.9) | copy-start | bytes 3145732
  210.1 168.8 %copy-start.4 = (bf16[256,2048]{1,0:T(8,128)(2,1)S(1)}, bf16[256,2048]{1,0:T(8,128)(2,1)}, u32[]{:S(2)}) copy-start(bf16[256,2048]{1,0:T(8,128)(2,1)} %param.11) | copy-start | bytes 3145732
  378.8 4.9 slice-start
  378.9 4.8 slice-start.1
  378.9 5.0 copy-start.1
  386.4 2.8 copy-start.3
  389.2 1.5 copy-start.5
Sparse Core Ops, SparseCore 0:
  13.6 180.6 all-gather.4
  199.8 168.8 all-gather.6
  401.2 203.0 all-reduce.2

commit v2 on v1

v2 whole, which is shorter than its diff:
```python
import functools

import jax
import jax.numpy as jnp
from jax import lax
from jax.experimental import pallas as pl
from jax.experimental.pallas import tpu as pltpu
from jax.sharding import PartitionSpec as P

MESH = pl.DeviceIdType.MESH
F32 = jnp.float32
BF16 = jnp.bfloat16
LEAD = 20
PIECES = 10


def offset_of(j):
    odd = j % 2
    return (j // 2) * (1 - odd) - ((j + 1) // 2) * odd


def kernel(
    dims, tok, cot, lev, gate_w, up_w, down_w,
    mixed_out, grad_out, gu_out, down_out,
    r_tok, r_cot, stage, gath, gw, uw, dw, dwt, acc, gv, uv, hg, act, act_t,
    part, part_send, part_recv, sx, rx, syf, sy, ry,
    w_sem, p0_send, p0_recv, ring_recv, sib_recv, main_send, p1_send, rs_send, rs1_recv, rsx_recv, rsy_recv,
):
    nx, ny, nz, units, width, ff = dims
    hy, hz = ny // 2, nz // 2
    z = lax.axis_index("dp")
    t = lax.axis_index("tensor")
    x = t // (ny * 2)
    y = (t // 2) % ny
    c = t % 2
    rank = x * 2 + c
    colour = width // 2
    z_slots = (hz + 1) * ny
    y_slots = (nz // 4) * (hy + 1) * 4
    chunks = nz // 2

    def dev(zz, xx, yy, cc):
        return {"dp": zz, "tensor": (xx * ny + yy) * 2 + cc}

    copies = [
        pltpu.make_async_copy(gate_w, gw, w_sem.at[0]),
        pltpu.make_async_copy(up_w, uw, w_sem.at[1]),
        pltpu.make_async_copy(down_w, dw, w_sem.at[2]),
    ]
    for copy in copies:
        copy.start()

    barrier = pltpu.get_barrier_semaphore()
    greeted = 0
    for d in range(1, nx):
        for e in range(2):
            pl.semaphore_signal(barrier, inc=1, device_id=dev(z, (x + d) % nx, y, e), device_id_type=MESH)
            greeted += 1
    pl.semaphore_signal(barrier, inc=1, device_id=dev(z, x, y, 1 - c), device_id_type=MESH)
    greeted += 1
    for d in range(1, ny):
        pl.semaphore_signal(barrier, inc=1, device_id=dev(z, x, (y + d) % ny, c), device_id_type=MESH)
        greeted += 1
    for d in (1, nz - 1):
        pl.semaphore_signal(barrier, inc=1, device_id=dev((z + d) % nz, x, y, c), device_id_type=MESH)
        greeted += 1

    def clear(r, carry):
        acc[pl.ds(r * 8, 8), :] = jnp.zeros((8, width), F32)
        return carry

    lax.fori_loop(0, 3 * units // 8, clear, 0)
    pl.semaphore_wait(barrier, greeted)

    def p0(src, landing, which, slot, sem_slot, target):
        return pltpu.make_async_remote_copy(
            src_ref=src, dst_ref=landing.at[slot], send_sem=p0_send.at[which, sem_slot],
            recv_sem=p0_recv.at[which, slot], device_id=target, device_id_type=MESH,
        )

    for which, (src, landing) in enumerate(((tok, r_tok), (cot, r_cot))):
        pltpu.make_async_copy(src, landing.at[rank], p0_recv.at[which, rank]).start()
        for d in range(1, 2 * nx):
            other = (rank + d) % (2 * nx)
            p0(src, landing, which, rank, d, dev(z, other // 2, y, other % 2)).start()
    for which, (src, landing) in enumerate(((tok, r_tok), (cot, r_cot))):
        pltpu.make_async_copy(src, landing.at[rank], p0_recv.at[which, rank]).wait()
        for d in range(1, 2 * nx):
            other = (rank + d) % (2 * nx)
            p0(src, landing, which, other, d, dev(z, other // 2, y, other % 2)).wait_recv()
        for k in range(2 * nx):
            stage[2 * k:2 * k + 2, :] = landing[k].astype(F32)
        gath[z, y, :, which * width:(which + 1) * width] = stage[...].astype(BF16)

    def block(col, zz, yy, half):
        start = pl.multiple_of(half * width + col * colour, 128)
        return gath.at[zz, yy, :, pl.ds(start, colour)]

    def ring(col, zz, yy, target, send_sem):
        return pltpu.make_async_remote_copy(
            src_ref=block(col, zz, yy, c), dst_ref=block(col, zz, yy, c), send_sem=send_sem,
            recv_sem=ring_recv.at[col, zz, yy], device_id=target, device_id_type=MESH,
        )

    def sibling(col, zz, yy, half, send_sem):
        return pltpu.make_async_remote_copy(
            src_ref=block(col, zz, yy, half), dst_ref=block(col, zz, yy, half), send_sem=send_sem,
            recv_sem=sib_recv.at[col, zz, yy], device_id=dev(z, x, y, 1 - c), device_id_type=MESH,
        )

    z_next, z_prev = (z + 1) % nz, (z + nz - 1) % nz
    y_next, y_prev = (y + 1) % ny, (y + ny - 1) % ny
    to_z = (dev(z_next, x, y, c), dev(z_prev, x, y, c))
    to_y = (dev(z, x, y_next, c), dev(z, x, y_prev, c))

    def p1_block(stream, k):
        if stream == 0:
            return 0, z, (y + ny - k) % ny, to_y[0], hy
        if stream == 1:
            return 0, z, (y + k) % ny, to_y[1], ny - 1 - hy
        if stream == 2:
            return 1, (z + nz - k) % nz, y, to_z[0], hz
        return 1, (z + k) % nz, y, to_z[1], nz - 1 - hz

    def p1_step(k):
        for stream in range(4):
            col, zz, yy, target, last = p1_block(stream, k)

            @pl.when(k <= last)
            def _():
                ring(col, zz, yy, target, p1_send.at[stream, k]).wait_recv()
                sibling(col, zz, yy, c, p1_send.at[4 + stream, k]).start()

            @pl.when(k < last)
            def _():
                ring(col, zz, yy, target, p1_send.at[stream, k]).start()

    def p1_drain(k):
        for stream in range(4):
            col, zz, yy, target, last = p1_block(stream, k)

            @pl.when(k < last)
            def _():
                ring(col, zz, yy, target, p1_send.at[stream, k]).wait_send()

            @pl.when((k >= 1) & (k <= last))
            def _():
                sibling(col, zz, yy, c, p1_send.at[4 + stream, k]).wait_send()

    def main_block(stream, i):
        down = stream % 2
        if stream < 2:
            s, j = i // ny, i % ny
            yy = (y + offset_of(j) + ny) % ny
            zz = (z + s) % nz if down else (z + nz - s) % nz
            mine = (j >= ny // 2) if down else (j < ny // 2)
            live, half = i < z_slots, hz
            target, col = to_z[down], 0
        else:
            g, s, jj = i // ((hy + 1) * 4), (i // 4) % (hy + 1), i % 4
            zz = (z + offset_of(g * 4 + jj) + nz) % nz
            yy = (y + s) % ny if down else (y + ny - s) % ny
            mine = (jj >= 2) if down else (jj < 2)
            live, half = i < y_slots, hy
            target, col = to_y[down], 1
        arrives = live & (s >= 1) & ((s < half) | mine)
        forwards = live & ((s < half - 1) | ((s == half - 1) & mine))
        return col, zz, yy, target, arrives, forwards

    def main_slot(i):
        for stream in range(4):
            col, zz, yy, target, arrives, forwards = main_block(stream, i)

            @pl.when(arrives)
            def _():
                ring(col, zz, yy, target, main_send.at[stream, i]).wait_recv()

            @pl.when(forwards)
            def _():
                ring(col, zz, yy, target, main_send.at[stream, i]).start()

            @pl.when(arrives)
            def _():
                sibling(col, zz, yy, c, main_send.at[4 + stream, i]).start()

    def main_drain(i):
        for stream in range(4):
            col, zz, yy, target, arrives, forwards = main_block(stream, i)

            @pl.when(forwards)
            def _():
                ring(col, zz, yy, target, main_send.at[stream, i]).wait_send()

            @pl.when(arrives)
            def _():
                sibling(col, zz, yy, c, main_send.at[4 + stream, i]).wait_send()

    for stream in range(4):
        col, zz, yy, target, last = p1_block(stream, 0)
        ring(col, zz, yy, target, p1_send.at[stream, 0]).start()

    for copy in copies:
        copy.wait()
    dwt[...] = dw[...].T

    rows = ny * 16

    def groups_of(m):
        return (z + m) % nz, (z + nz - m - 1) % nz

    def pair(m, half):
        first, second = groups_of(m)
        top = gath[first, :, :, half * width:(half + 1) * width].reshape(rows, width)
        low = gath[second, :, :, half * width:(half + 1) * width].reshape(rows, width)
        return jnp.concatenate([top, low], axis=0)

    def wait_partner(m):
        def step(yy, carry):
            for zz in groups_of(m):
                @pl.when((zz != z) | (yy != y))
                def _():
                    for col in range(2):
                        sibling(col, zz, yy, 1 - c, p1_send.at[0, 0]).wait_recv()
            return carry

        lax.fori_loop(0, ny, step, 0)

    strip = rows // 2

    def gates(m):
        first, second = groups_of(m)

        def step(r, carry):
            here = pl.ds(pl.multiple_of(r * strip, strip), strip)
            group = jnp.where(r < 2, first, second)
            unit = t * units + lax.broadcasted_iota(jnp.int32, (strip, units), 1)
            live = unit < lax.shift_right_arithmetic(jnp.int32(ff), lev[group])
            gate, up = gv[here, :], uv[here, :]
            grad = jnp.where(live, hg[here, :], 0.0)
            sig = 1.0 / (1.0 + jnp.exp(-gate))
            act[here, 2 * units:3 * units] = jnp.where(live, gate * sig * up, 0.0).astype(BF16)
            act[here, 0:units] = (grad * up * sig * (1.0 + gate * (1.0 - sig))).astype(BF16)
            act[here, units:2 * units] = (grad * gate * sig).astype(BF16)
            return carry

        lax.fori_loop(0, 4, step, 0)
        for k in range(3):
            act_t[k * units:(k + 1) * units, :] = act[:, k * units:(k + 1) * units].T

    def weight_piece(m, q):
        k, side = q // 2, q % 2
        cols = slice(side * colour, (side + 1) * colour)
        first, second = groups_of(m)
        half = 1 if k == 2 else 0
        span = slice(half * width + side * colour, half * width + (side + 1) * colour)
        value = jnp.concatenate(
            [gath[first, :, :, span].reshape(rows, colour), gath[second, :, :, span].reshape(rows, colour)], axis=0
        )
        total = acc[k * units:(k + 1) * units, cols] + jnp.dot(
            act_t[k * units:(k + 1) * units, :], value, preferred_element_type=F32
        )

        @pl.when(m < chunks - 1)
        def _():
            acc[k * units:(k + 1) * units, cols] = total

        @pl.when(m == chunks - 1)
        def _():
            if k < 2:
                gu_out[k * units:(k + 1) * units, cols] = total.astype(BF16)
            else:
                down_out[:, cols] = total.astype(BF16)

    def piece(m, q):
        if q == 0:
            wait_partner(m)
            gv[...] = jnp.dot(pair(m, 0), gw[...], preferred_element_type=F32)
        elif q == 1:
            uv[...] = jnp.dot(pair(m, 0), uw[...], preferred_element_type=F32)
        elif q == 2:
            hg[...] = jnp.dot(pair(m, 1), dwt[...], preferred_element_type=F32)
        elif q == 3:
            gates(m)
        else:
            weight_piece(m, q - 4)

    def ordered(k):
        to = lax.broadcasted_iota(jnp.int32, (rows, rows), 0)
        src = lax.broadcasted_iota(jnp.int32, (rows, rows), 1)
        per_x = 2 * ny
        core, rest = to // (nx * per_x), to % (nx * per_x)
        xx, low = rest // per_x, rest % per_x
        origin = (low // 2) * (4 * nx) + xx * 4 + core * 2 + low % 2
        pick = (origin == src).astype(F32).astype(BF16)
        return jnp.dot(pick, act[0:rows, k * units:(k + 1) * units], preferred_element_type=F32).astype(BF16)

    def partner_part():
        return pltpu.make_async_remote_copy(
            src_ref=part_send, dst_ref=part_recv, send_sem=rs_send.at[0], recv_sem=rs1_recv,
            device_id=dev(z, x, y, 1 - c), device_id_type=MESH,
        )

    def x_part(d, slot):
        other = (x + d) % nx
        return pltpu.make_async_remote_copy(
            src_ref=sx.at[other], dst_ref=rx.at[slot], send_sem=rs_send.at[d],
            recv_sem=rsx_recv.at[slot], device_id=dev(z, other, y, c), device_id_type=MESH,
        )

    def y_part(d, slot):
        other = (y + d) % ny
        return pltpu.make_async_remote_copy(
            src_ref=sy.at[other], dst_ref=ry.at[slot], send_sem=rs_send.at[nx + d],
            recv_sem=rsy_recv.at[slot], device_id=dev(z, x, other, c), device_id_type=MESH,
        )

    nt = (((1,), (1,)), ((), ()))

    def outputs(i):
        @pl.when(i == LEAD + PIECES)
        def _():
            value = jnp.dot(ordered(2), dw[...], preferred_element_type=F32)
            part[:, :, 0:width] = value.reshape(2, rows // 2, width)

        @pl.when(i == LEAD + PIECES + 1)
        def _():
            value = lax.dot_general(ordered(0), gw[...], nt, preferred_element_type=F32)
            value = value + lax.dot_general(ordered(1), uw[...], nt, preferred_element_type=F32)
            part[:, :, width:2 * width] = value.reshape(2, rows // 2, width)

        @pl.when(i == LEAD + PIECES + 2)
        def _():
            part_send[...] = part[1 - c].astype(BF16)
            partner_part().start()

        @pl.when(i == LEAD + PIECES + 10)
        def _():
            partner_part().wait_recv()
            part[c] = part[c] + part_recv[...].astype(F32)
            sx[...] = part[c].astype(BF16).reshape(nx, 2 * ny, 2 * width)
            for d in range(1, nx):
                x_part(d, x).start()

        @pl.when(i == LEAD + PIECES + 20)
        def _():
            total = part[c, pl.ds(pl.multiple_of(x * 2 * ny, 2 * ny), 2 * ny), :]
            for d in range(1, nx):
                x_part(d, (x + d) % nx).wait_recv()
                total = total + rx[(x + d) % nx].astype(F32)
            for k in range(ny):
                syf[k] = total[2 * k:2 * k + 2, :]
                sy[k] = total[2 * k:2 * k + 2, :].astype(BF16)
            for d in range(1, ny):
                y_part(d, y).start()

        @pl.when(i == LEAD + PIECES + 30)
        def _():
            total = syf[y]
            for d in range(1, ny):
                y_part(d, (y + d) % ny).wait_recv()
                total = total + ry[(y + d) % ny].astype(F32)
            mixed_out[...] = total[:, 0:width].astype(BF16)
            grad_out[...] = total[:, width:2 * width].astype(BF16)

    slots = max(LEAD + PIECES * chunks, LEAD + PIECES + 31, z_slots, y_slots)

    def slot(i, carry):
        @pl.when((i % 2 == 1) & (i < 2 * max(hy, hz)))
        def _():
            p1_step((i + 1) // 2)

        main_slot(i)
        m = i // PIECES - LEAD // PIECES
        for q in range(PIECES):
            @pl.when((i % PIECES == q) & (m >= 0) & (m < chunks))
            def _():
                piece(m, q)

        outputs(i)
        return carry

    lax.fori_loop(0, slots, slot, 0)

    for which, (src, landing) in enumerate(((tok, r_tok), (cot, r_cot))):
        for d in range(1, 2 * nx):
            other = (rank + d) % (2 * nx)
            p0(src, landing, which, rank, d, dev(z, other // 2, y, other % 2)).wait_send()

    def drain_p1(k, carry):
        p1_drain(k)
        return carry

    lax.fori_loop(0, max(hy, hz) + 1, drain_p1, 0)

    def drain_main(i, carry):
        main_drain(i)
        return carry

    lax.fori_loop(0, max(z_slots, y_slots), drain_main, 0)
    partner_part().wait_send()
    for d in range(1, nx):
        x_part(d, x).wait_send()
    for d in range(1, ny):
        y_part(d, y).wait_send()


def make_body(nx, ny, nz, ff):
    def body(tokens, cotangent, levels, gate_weight, up_weight, down_weight):
        width, units = gate_weight.shape
        rows = ny * 16
        slots = max((nz // 2 + 1) * ny, (nz // 4) * (ny // 2 + 1) * 4)
        vmem = pl.BlockSpec(memory_space=pltpu.VMEM)
        hbm = pl.BlockSpec(memory_space=pl.ANY)
        dma = pltpu.SemaphoreType.DMA
        mixed, grad, gu, down = pl.pallas_call(
            functools.partial(kernel, (nx, ny, nz, units, width, ff)),
            out_shape=(
                jax.ShapeDtypeStruct((2, width), BF16),
                jax.ShapeDtypeStruct((2, width), BF16),
                jax.ShapeDtypeStruct((2 * units, width), BF16),
                jax.ShapeDtypeStruct((units, width), BF16),
            ),
            in_specs=[vmem, vmem, pl.BlockSpec(memory_space=pltpu.SMEM), hbm, hbm, hbm],
            out_specs=(vmem, vmem, vmem, vmem),
            scratch_shapes=[
                pltpu.VMEM((2 * nx, 2, width), BF16),
                pltpu.VMEM((2 * nx, 2, width), BF16),
                pltpu.VMEM((4 * nx, width), F32),
                pltpu.VMEM((nz, ny, 16, 2 * width), BF16),
                pltpu.VMEM((width, units), BF16),
                pltpu.VMEM((width, units), BF16),
                pltpu.VMEM((units, width), BF16),
                pltpu.VMEM((width, units), BF16),
                pltpu.VMEM((3 * units, width), F32),
                pltpu.VMEM((2 * rows, units), F32),
                pltpu.VMEM((2 * rows, units), F32),
                pltpu.VMEM((2 * rows, units), F32),
                pltpu.VMEM((2 * rows, 3 * units), BF16),
                pltpu.VMEM((3 * units, 2 * rows), BF16),
                pltpu.VMEM((2, rows // 2, 2 * width), F32),
                pltpu.VMEM((rows // 2, 2 * width), BF16),
                pltpu.VMEM((rows // 2, 2 * width), BF16),
                pltpu.VMEM((nx, 2 * ny, 2 * width), BF16),
                pltpu.VMEM((nx, 2 * ny, 2 * width), BF16),
                pltpu.VMEM((ny, 2, 2 * width), F32),
                pltpu.VMEM((ny, 2, 2 * width), BF16),
                pltpu.VMEM((ny, 2, 2 * width), BF16),
                dma((3,)),
                dma((2, 2 * nx)),
                dma((2, 2 * nx)),
                dma((2, nz, ny)),
                dma((2, nz, ny)),
                dma((8, slots)),
                dma((8, max(nz, ny) // 2 + 1)),
                dma((nx + ny,)),
                dma,
                dma((nx,)),
                dma((ny,)),
            ],
            compiler_params=pltpu.CompilerParams(
                collective_id=0, has_side_effects=True, vmem_limit_bytes=60 * 1024 * 1024
            ),
        )(tokens, cotangent, levels, gate_weight, up_weight, down_weight)
        return mixed, grad, gu[:units].T, gu[units:].T, down

    return body


def solution(mesh):
    rows = P(("dp", "tensor"), None)
    columns = P(None, "tensor")
    units = P("tensor", None)
    return jax.shard_map(
        make_body(4, mesh.shape["tensor"] // 8, mesh.shape["dp"], 16384),
        mesh=mesh,
        in_specs=(rows, rows, P(), columns, columns, units),
        out_specs=(rows, rows, columns, columns, units),
        check_vma=False,
    )
```

time: 614 us -> 121 us (0.20)
  waiting for transfers between devices: 540 us -> 0 us
  Pallas kernels: 0 us -> 114 us
  matrix products: 27.6 us -> 0 us
  local copies, waits for them, and re-layouts: 27.9 us -> 6.51 us
  between operations: 14.5 us -> 0.68 us
    all_gather x2 -> x0, waiting for transfers between devices: 341 us -> none  [the longest x1 183 us: body(): all_tokens = lax.all_gather(tokens, ('dp', 'tensor'), axis=0, tiled=True)]
    unnamed x4 -> x0, waiting for transfers between devices: 199 us -> none
    pallas_call x0 -> x1, Pallas kernels: none -> 114 us  [body(): pl.pallas_call(functools.partial(kernel, (nx, ny, nz, units, width, ff)),...]
    dot_general x9 -> x0, matrix products: 27.6 us -> none  [the longest x1 5.74 us: body(): jnp.dot(all_tokens, gate_weight, preferred_element_type=jnp.float32)]
    unnamed x21 -> x11, local copies, waits for them, and re-layouts: 26.3 us -> 4.79 us
  transfers between devices with their start and end apart: 3 -> 0, of which waited for: 3 -> 0; matrix products, arithmetic and copies ran while one was open for 4% -> 0% of each run, Pallas kernels for 0% -> 0%
where the time goes in v2:
time: 121 us
  Pallas kernels  114 us (94%)
  local copies, waits for them, and re-layouts  6.51 us (5%)
    pallas_call x1, Pallas kernels, body(): pl.pallas_call(functools.partial(kernel, (nx, ny, nz, units, width, ff)),...  114 us
    unnamed x11, local copies, waits for them, and re-layouts  4.79 us

profile of v2, /device:TPU:1, one launch (start us, length us, event | category | flops | bytes accessed | tf_op | source)
XLA Modules:
  0.0 121.3 jit_solution(17180852015822464451)
XLA Ops:
  0.6 114.1 %shard_map.101 = (bf16[2,2048]{1,0:T(2,128)(2,1)}, bf16[2,2048]{1,0:T(2,128)(2,1)}, bf16[512,2048]{1,0:T(8,128)(2,1)}, bf16[256,2048]{1,0:T(8,128)(2,1)}) custom-call(bf16[2,2048]{1,0:T(2,128)(2,1)} %tok.1, bf16[2,2048]{1,0:T(2,128)(2,1)} %cot.1, s32[12]{0:T(128)} %lev.1, bf16[2048,256]{1,0:T(8,128)(2,1)} %gate_w.1, bf16[2048,256]{1,0:T(8,128)(2,1)} %up_w.1, ...), custom_call_target="tpu_custom_call" | custom-call | tf_op jit(solution)/shard_map/pallas_call | solution.py:415
  114.7 1.7 %slice_bitcast_fusion = (bf16[2048,256]{0,1:T(8,128)(2,1)S(1)}, bf16[2048,256]{0,1:T(8,128)(2,1)S(1)}) fusion(bf16[512,2048]{1,0:T(8,128)(2,1)} %get-tuple-element.11), kind=kLoop, calls=%fused_computation | loop fusion | bytes 4194304 | tf_op jit(solution)/shard_map/transpose | solution.py:464
  116.5 0.0 copy-start.2
  116.5 0.0 copy-start.1
  116.5 0.0 copy-start
  116.5 1.3 %copy.12 = bf16[2048,256]{1,0:T(8,128)(2,1)} copy(bf16[2048,256]{0,1:T(8,128)(2,1)S(1)} %get-tuple-element.18) | data formatting | bytes 2097152
  117.8 1.3 %copy.11 = bf16[2048,256]{1,0:T(8,128)(2,1)} copy(bf16[2048,256]{0,1:T(8,128)(2,1)S(1)} %get-tuple-element.19) | data formatting | bytes 2097152
  119.1 0.0 copy-done.2
  119.1 0.6 copy.16
  119.7 0.0 copy-done.1
  119.7 0.6 copy.17
  120.3 0.0 copy-done
  120.3 1.0 copy.18
Async XLA Ops:
  116.5 2.6 %copy-start.2 = (bf16[2,2048]{1,0:T(2,128)(2,1)S(1)}, bf16[2,2048]{1,0:T(2,128)(2,1)}, u32[]{:S(2)}) copy-start(bf16[2,2048]{1,0:T(2,128)(2,1)} %get-tuple-element.25) | copy-start | bytes 24580
  116.5 3.2 %copy-start.1 = (bf16[2,2048]{1,0:T(2,128)(2,1)S(1)}, bf16[2,2048]{1,0:T(2,128)(2,1)}, u32[]{:S(2)}) copy-start(bf16[2,2048]{1,0:T(2,128)(2,1)} %get-tuple-element.26) | copy-start | bytes 24580
  116.5 3.8 %copy-start = (bf16[256,2048]{1,0:T(8,128)(2,1)S(1)}, bf16[256,2048]{1,0:T(8,128)(2,1)}, u32[]{:S(2)}) copy-start(bf16[256,2048]{1,0:T(8,128)(2,1)} %get-tuple-element.29) | copy-start | bytes 3145732

commit v3 on v2

v3 whole, which is shorter than its diff:
```python
import functools

import jax
import jax.numpy as jnp
from jax import lax
from jax.experimental import pallas as pl
from jax.experimental.pallas import tpu as pltpu
from jax.sharding import PartitionSpec as P

MESH = pl.DeviceIdType.MESH
F32 = jnp.float32
BF16 = jnp.bfloat16
LEAD = 6
PIECES = 7


def wrap(v, n):
    v = jnp.where(v < 0, v + n, v)
    return jnp.where(v >= n, v - n, v)


def kernel(
    dims, tok, cot, lev, gate_w, up_w, down_w,
    mixed_out, grad_out, gate_out, up_out, down_out,
    r_tok, r_cot, stage, gath, gu, dw, dwt, acc, guv, hg, act, act_t,
    part, part_send, part_recv, sx, rx, syf, sy, ry,
    w_sem, p0_send, p0_recv, ring_recv, sib_recv, sib_send, main_send, p1_send, rs_send, rs1_recv, rsx_recv, rsy_recv,
):
    nx, ny, nz, units, width, ff = dims
    hy, hz = ny // 2, nz // 2
    z = lax.axis_index("dp")
    t = lax.axis_index("tensor")
    x = t // (ny * 2)
    y = (t // 2) % ny
    c = t % 2
    rank = x * 2 + c
    colour = width // 2
    chunks = nz // 2

    def dev(zz, xx, yy, cc):
        return {"dp": zz, "tensor": (xx * ny + yy) * 2 + cc}

    copies = [
        pltpu.make_async_copy(gate_w, gu.at[:, 0:units], w_sem.at[0]),
        pltpu.make_async_copy(up_w, gu.at[:, units:2 * units], w_sem.at[1]),
        pltpu.make_async_copy(down_w, dw, w_sem.at[2]),
    ]
    for copy in copies:
        copy.start()

    barrier = pltpu.get_barrier_semaphore()
    greeted = 0
    for d in range(1, nx):
        for e in range(2):
            pl.semaphore_signal(barrier, inc=1, device_id=dev(z, wrap(x + d, nx), y, e), device_id_type=MESH)
            greeted += 1
    pl.semaphore_signal(barrier, inc=1, device_id=dev(z, x, y, 1 - c), device_id_type=MESH)
    greeted += 1
    for d in range(1, ny):
        pl.semaphore_signal(barrier, inc=1, device_id=dev(z, x, wrap(y + d, ny), c), device_id_type=MESH)
        greeted += 1
    for d in (1, nz - 1):
        pl.semaphore_signal(barrier, inc=1, device_id=dev(wrap(z + d, nz), x, y, c), device_id_type=MESH)
        greeted += 1

    def clear(r, carry):
        acc[pl.ds(r * 8, 8), :] = jnp.zeros((8, width), F32)
        return carry

    lax.fori_loop(0, 3 * units // 8, clear, 0)
    pl.semaphore_wait(barrier, greeted)

    def p0(src, landing, which, slot, sem_slot, target):
        return pltpu.make_async_remote_copy(
            src_ref=src, dst_ref=landing.at[slot], send_sem=p0_send.at[which, sem_slot],
            recv_sem=p0_recv.at[which, slot], device_id=target, device_id_type=MESH,
        )

    for which, (src, landing) in enumerate(((tok, r_tok), (cot, r_cot))):
        pltpu.make_async_copy(src, landing.at[rank], p0_recv.at[which, rank]).start()
        for d in range(1, 2 * nx):
            other = wrap(rank + d, 2 * nx)
            p0(src, landing, which, rank, d, dev(z, other // 2, y, other % 2)).start()
    for which, (src, landing) in enumerate(((tok, r_tok), (cot, r_cot))):
        pltpu.make_async_copy(src, landing.at[rank], p0_recv.at[which, rank]).wait()
        for d in range(1, 2 * nx):
            other = wrap(rank + d, 2 * nx)
            p0(src, landing, which, other, d, dev(z, other // 2, y, other % 2)).wait_recv()
        for k in range(2 * nx):
            stage[2 * k:2 * k + 2, :] = landing[k].astype(F32)
        gath[z, y, :, which * width:(which + 1) * width] = stage[...].astype(BF16)

    def block(col, zz, yy, half):
        start = pl.multiple_of(half * width + col * colour, 128)
        return gath.at[zz, yy, :, pl.ds(start, colour)]

    def ring(col, zz, yy, target, send_sem):
        return pltpu.make_async_remote_copy(
            src_ref=block(col, zz, yy, c), dst_ref=block(col, zz, yy, c), send_sem=send_sem,
            recv_sem=ring_recv.at[col, zz, yy], device_id=target, device_id_type=MESH,
        )

    def sibling(col, zz, yy, m):
        return pltpu.make_async_remote_copy(
            src_ref=block(col, zz, yy, c), dst_ref=block(col, zz, yy, c), send_sem=sib_send,
            recv_sem=sib_recv.at[m], device_id=dev(z, x, y, 1 - c), device_id_type=MESH,
        )

    z_next, z_prev = wrap(z + 1, nz), wrap(z - 1, nz)
    y_next, y_prev = wrap(y + 1, ny), wrap(y - 1, ny)
    to_z = (dev(z_next, x, y, c), dev(z_prev, x, y, c))
    to_y = (dev(z, x, y_next, c), dev(z, x, y_prev, c))

    def p1_block(stream, k):
        if stream == 0:
            return 0, z, wrap(y - k, ny), to_y[0], hy, 0
        if stream == 1:
            return 0, z, wrap(y + k, ny), to_y[1], ny - 1 - hy, 0
        if stream == 2:
            return 1, wrap(z - k, nz), y, to_z[0], hz, k - 1
        return 1, wrap(z + k, nz), y, to_z[1], nz - 1 - hz, k

    def p1_step(k):
        for stream in range(4):
            col, zz, yy, target, last, m = p1_block(stream, k)

            @pl.when(k <= last)
            def _():
                ring(col, zz, yy, target, p1_send.at[stream, k]).wait_recv()

                @pl.when(k < last)
                def _():
                    ring(col, zz, yy, target, p1_send.at[stream, k]).start()

                sibling(col, zz, yy, m).start()

    def main_slot(t, r):
        for axis in range(2):
            side, far = (hy, hz) if axis == 0 else (hz, hy)
            d, s = (r, t - r) if axis == 0 else (t - r, r)
            for e in range(2):
                live = (s >= 0) & (s <= far) & (((d >= 0) & (d <= side)) if e == 0 else ((d >= 1) & (d < side)))
                for down in range(2):
                    across = d if e else -d
                    along = s if down else -s
                    if axis == 0:
                        zz, yy, target = wrap(z + along, nz), wrap(y + across, ny), to_z[down]
                        m = s if down else s - 1
                        m = jnp.where(s == hz, chunks - 1, jnp.maximum(m, 0))
                    else:
                        zz, yy, target = wrap(z + across, nz), wrap(y + along, ny), to_y[down]
                        m = d if e else jnp.maximum(d - 1, 0)
                    if e == 1:
                        mine = down == 1
                        arrives = live & (s >= 1) & (s < far + down)
                        forwards = live & (s < far - 1 + down)
                    else:
                        mine = (d == side) if down else (d < side)
                        arrives = live & (s >= 1) & ((s < far) | mine)
                        forwards = live & ((s < far - 1) | ((s == far - 1) & mine))
                    copy = functools.partial(ring, axis, zz, yy, target, main_send.at[2 * axis + down])

                    @pl.when(arrives)
                    def _():
                        copy().wait_recv()

                    @pl.when(forwards)
                    def _():
                        copy().start()

                    @pl.when(arrives)
                    def _():
                        sibling(axis, zz, yy, m).start()

    for stream in range(4):
        col, zz, yy, target, last, m = p1_block(stream, 0)
        ring(col, zz, yy, target, p1_send.at[stream, 0]).start()

    for copy in copies:
        copy.wait()
    dwt[...] = dw[...].T

    rows = ny * 16

    def groups_of(m):
        return wrap(z + m, nz), wrap(z - m - 1, nz)

    def pair(m, half):
        first, second = groups_of(m)
        top = gath[first, :, :, half * width:(half + 1) * width].reshape(rows, width)
        low = gath[second, :, :, half * width:(half + 1) * width].reshape(rows, width)
        return jnp.concatenate([top, low], axis=0)

    def bytes_of(blocks, sem):
        span = acc.at[0:blocks * 4, :]
        return pltpu.make_async_copy(span, span, sem)

    def wait_partner(m):
        @pl.when(m == 0)
        def _():
            bytes_of(4 * ny - 2, sib_recv.at[0]).wait()

        @pl.when(m > 0)
        def _():
            bytes_of(4 * ny, sib_recv.at[m]).wait()

    strip = rows // 2

    def gates(m):
        first, second = groups_of(m)

        def step(r, carry):
            here = pl.ds(pl.multiple_of(r * strip, strip), strip)
            group = jnp.where(r < 2, first, second)
            unit = t * units + lax.broadcasted_iota(jnp.int32, (strip, units), 1)
            live = unit < lax.shift_right_arithmetic(jnp.int32(ff), lev[group])
            gate, up = guv[here, 0:units], guv[here, units:2 * units]
            grad = jnp.where(live, hg[here, :], 0.0)
            sig = 1.0 / (1.0 + jnp.exp(-gate))
            act[here, 2 * units:3 * units] = jnp.where(live, gate * sig * up, 0.0).astype(BF16)
            act[here, 0:units] = (grad * up * sig * (1.0 + gate * (1.0 - sig))).astype(BF16)
            act[here, units:2 * units] = (grad * gate * sig).astype(BF16)
            return carry

        lax.fori_loop(0, 4, step, 0)
        for k in range(3):
            act_t[k * units:(k + 1) * units, :] = act[:, k * units:(k + 1) * units].T

    def weight_piece(m, side, down):
        cols = slice(side * colour, (side + 1) * colour)
        first, second = groups_of(m)
        span = slice(down * width + side * colour, down * width + (side + 1) * colour)
        value = jnp.concatenate(
            [gath[first, :, :, span].reshape(rows, colour), gath[second, :, :, span].reshape(rows, colour)], axis=0
        )
        lines = slice(2 * units, 3 * units) if down else slice(0, 2 * units)
        total = acc[lines, cols] + jnp.dot(act_t[lines, :], value, preferred_element_type=F32)

        @pl.when(m < chunks - 1)
        def _():
            acc[lines, cols] = total

        @pl.when(m == chunks - 1)
        def _():
            if down:
                down_out[:, cols] = total.astype(BF16)
            else:
                gate_out[:, cols] = total[0:units].astype(BF16)
                up_out[:, cols] = total[units:2 * units].astype(BF16)

    def piece(m, q):
        if q == 0:
            wait_partner(m)
            guv[...] = jnp.dot(pair(m, 0), gu[...], preferred_element_type=F32)
        elif q == 1:
            hg[...] = jnp.dot(pair(m, 1), dwt[...], preferred_element_type=F32)
        elif q == 2:
            gates(m)
        else:
            weight_piece(m, (q - 3) % 2, (q - 3) // 2)

    def ordered(k):
        to = lax.broadcasted_iota(jnp.int32, (rows, rows), 0)
        src = lax.broadcasted_iota(jnp.int32, (rows, rows), 1)
        bits_x, bits_y = nx.bit_length() - 1, ny.bit_length() - 1

        def part_of(value, low, bits):
            return jnp.bitwise_and(jnp.right_shift(value, low), (1 << bits) - 1)

        row, yy = part_of(to, 0, 1), part_of(to, 1, bits_y)
        xx, core = part_of(to, 1 + bits_y, bits_x), part_of(to, 1 + bits_y + bits_x, 1)
        origin = yy * (4 * nx) + xx * 4 + core * 2 + row
        pick = (origin == src).astype(F32).astype(BF16)
        return jnp.dot(pick, act[0:rows, k * units:(k + 1) * units], preferred_element_type=F32).astype(BF16)

    def partner_part():
        return pltpu.make_async_remote_copy(
            src_ref=part_send, dst_ref=part_recv, send_sem=rs_send.at[0], recv_sem=rs1_recv,
            device_id=dev(z, x, y, 1 - c), device_id_type=MESH,
        )

    def x_part(d, slot):
        other = wrap(x + d, nx)
        return pltpu.make_async_remote_copy(
            src_ref=sx.at[other], dst_ref=rx.at[slot], send_sem=rs_send.at[d],
            recv_sem=rsx_recv.at[slot], device_id=dev(z, other, y, c), device_id_type=MESH,
        )

    def y_part(d, slot):
        other = wrap(y + d, ny)
        return pltpu.make_async_remote_copy(
            src_ref=sy.at[other], dst_ref=ry.at[slot], send_sem=rs_send.at[nx + d],
            recv_sem=rsy_recv.at[slot], device_id=dev(z, x, other, c), device_id_type=MESH,
        )

    nt = (((1,), (1,)), ((), ()))

    def outputs(t, r):
        @pl.when((t == LEAD + 1) & (r == 0))
        def _():
            value = jnp.dot(ordered(2), dw[...], preferred_element_type=F32)
            part[:, :, 0:width] = value.reshape(2, rows // 2, width)

        @pl.when((t == LEAD + 1) & (r == 1))
        def _():
            value = lax.dot_general(ordered(0), gu[:, 0:units], nt, preferred_element_type=F32)
            value = value + lax.dot_general(ordered(1), gu[:, units:2 * units], nt, preferred_element_type=F32)
            part[:, :, width:2 * width] = value.reshape(2, rows // 2, width)

        @pl.when((t == LEAD + 1) & (r == 2))
        def _():
            part_send[...] = part[1 - c].astype(BF16)
            partner_part().start()

        @pl.when((t == LEAD + 2) & (r == 3))
        def _():
            partner_part().wait_recv()
            part[c] = part[c] + part_recv[...].astype(F32)
            sx[...] = part[c].astype(BF16).reshape(nx, 2 * ny, 2 * width)
            for d in range(1, nx):
                x_part(d, x).start()

        @pl.when((t == LEAD + 4) & (r == 1))
        def _():
            total = part[c, pl.ds(pl.multiple_of(x * 2 * ny, 2 * ny), 2 * ny), :]
            for d in range(1, nx):
                x_part(d, wrap(x + d, nx)).wait_recv()
                total = total + rx[wrap(x + d, nx)].astype(F32)
            for k in range(ny):
                syf[k] = total[2 * k:2 * k + 2, :]
                sy[k] = total[2 * k:2 * k + 2, :].astype(BF16)
            for d in range(1, ny):
                y_part(d, y).start()

        @pl.when((t == LEAD + 5) & (r == 4))
        def _():
            total = syf[y]
            for d in range(1, ny):
                y_part(d, wrap(y + d, ny)).wait_recv()
                total = total + ry[wrap(y + d, ny)].astype(F32)
            mixed_out[...] = total[:, 0:width].astype(BF16)
            grad_out[...] = total[:, width:2 * width].astype(BF16)

    def wave(t, carry):
        @pl.when((t >= 1) & (t <= max(hy, hz)))
        def _():
            p1_step(t)

        def step(r, inner):
            @pl.when(r <= hy)
            def _():
                main_slot(t, r)

            m = t - LEAD
            for q in range(PIECES):
                @pl.when((r == q) & (m >= 0))
                def _():
                    piece(m, q)

            outputs(t, r)
            return inner

        lax.fori_loop(0, PIECES, step, 0)
        return carry

    lax.fori_loop(0, LEAD + chunks, wave, 0)

    for which, (src, landing) in enumerate(((tok, r_tok), (cot, r_cot))):
        for d in range(1, 2 * nx):
            other = wrap(rank + d, 2 * nx)
            p0(src, landing, which, rank, d, dev(z, other // 2, y, other % 2)).wait_send()

    def drain_p1(k, carry):
        for stream in range(4):
            col, zz, yy, target, last, m = p1_block(stream, k)

            @pl.when(k < last)
            def _():
                ring(col, zz, yy, target, p1_send.at[stream, k]).wait_send()
        return carry

    lax.fori_loop(0, max(hy, hz), drain_p1, 0)
    bytes_of(2 * (ny * nz - 1), sib_send).wait()
    for axis in range(2):
        side, far = (ny, hz) if axis == 0 else (nz, hy)
        for down in range(2):
            bytes_of(side * (far - 1) + side // 2, main_send.at[2 * axis + down]).wait()
    partner_part().wait_send()
    for d in range(1, nx):
        x_part(d, x).wait_send()
    for d in range(1, ny):
        y_part(d, y).wait_send()


def finish_kernel(mixed, grad, gate, up, down, *refs):
    outs, (mixed_v, grad_v, gate_v, up_v, down_v, gate_t, up_t, in_sem, out_sem) = refs[:5], refs[5:]
    landing = (mixed_v, grad_v, gate_v, up_v, down_v)
    leaving = (mixed_v, grad_v, gate_t, up_t, down_v)
    order = (2, 3, 4, 0, 1)
    units, width = gate_v.shape
    into = [pltpu.make_async_copy(a, b, in_sem.at[k]) for k, (a, b) in enumerate(zip((mixed, grad, gate, up, down), landing))]
    out = [pltpu.make_async_copy(a, b, out_sem.at[k]) for k, (a, b) in enumerate(zip(leaving, outs))]
    for k in order:
        into[k].start()
    for k in order:
        into[k].wait()
        if k in (2, 3):
            for b in range(width // units):
                span = slice(b * units, (b + 1) * units)
                leaving[k][span, :] = landing[k][:, span].T
        out[k].start()
    for k in order:
        out[k].wait()


def finish(mixed, grad, gate, up, down):
    units, width = gate.shape
    hbm = pl.BlockSpec(memory_space=pl.ANY)
    small, flat, tall = (2, width), (units, width), (width, units)
    return pl.pallas_call(
        finish_kernel,
        out_shape=tuple(jax.ShapeDtypeStruct(s, BF16) for s in (small, small, tall, tall, flat)),
        in_specs=[hbm] * 5,
        out_specs=(hbm,) * 5,
        scratch_shapes=[pltpu.VMEM(s, BF16) for s in (small, small, flat, flat, flat, tall, tall)]
        + [pltpu.SemaphoreType.DMA((5,)), pltpu.SemaphoreType.DMA((5,))],
    )(mixed, grad, gate, up, down)


def make_body(nx, ny, nz, ff):
    def body(tokens, cotangent, levels, gate_weight, up_weight, down_weight):
        width, units = gate_weight.shape
        rows = ny * 16
        vmem = pl.BlockSpec(memory_space=pltpu.VMEM)
        hbm = pl.BlockSpec(memory_space=pl.ANY)
        dma = pltpu.SemaphoreType.DMA
        mixed, grad, gate, up, down = pl.pallas_call(
            functools.partial(kernel, (nx, ny, nz, units, width, ff)),
            out_shape=(
                jax.ShapeDtypeStruct((2, width), BF16),
                jax.ShapeDtypeStruct((2, width), BF16),
                jax.ShapeDtypeStruct((units, width), BF16),
                jax.ShapeDtypeStruct((units, width), BF16),
                jax.ShapeDtypeStruct((units, width), BF16),
            ),
            in_specs=[vmem, vmem, pl.BlockSpec(memory_space=pltpu.SMEM), hbm, hbm, hbm],
            out_specs=(vmem, vmem, vmem, vmem, vmem),
            scratch_shapes=[
                pltpu.VMEM((2 * nx, 2, width), BF16),
                pltpu.VMEM((2 * nx, 2, width), BF16),
                pltpu.VMEM((4 * nx, width), F32),
                pltpu.VMEM((nz, ny, 16, 2 * width), BF16),
                pltpu.VMEM((width, 2 * units), BF16),
                pltpu.VMEM((units, width), BF16),
                pltpu.VMEM((width, units), BF16),
                pltpu.VMEM((3 * units, width), F32),
                pltpu.VMEM((2 * rows, 2 * units), F32),
                pltpu.VMEM((2 * rows, units), F32),
                pltpu.VMEM((2 * rows, 3 * units), BF16),
                pltpu.VMEM((3 * units, 2 * rows), BF16),
                pltpu.VMEM((2, rows // 2, 2 * width), F32),
                pltpu.VMEM((rows // 2, 2 * width), BF16),
                pltpu.VMEM((rows // 2, 2 * width), BF16),
                pltpu.VMEM((nx, 2 * ny, 2 * width), BF16),
                pltpu.VMEM((nx, 2 * ny, 2 * width), BF16),
                pltpu.VMEM((ny, 2, 2 * width), F32),
                pltpu.VMEM((ny, 2, 2 * width), BF16),
                pltpu.VMEM((ny, 2, 2 * width), BF16),
                dma((3,)),
                dma((2, 2 * nx)),
                dma((2, 2 * nx)),
                dma((2, nz, ny)),
                dma((nz // 2,)),
                dma,
                dma((4,)),
                dma((4, max(nz, ny) // 2 + 1)),
                dma((nx + ny,)),
                dma,
                dma((nx,)),
                dma((ny,)),
            ],
            compiler_params=pltpu.CompilerParams(
                collective_id=0, has_side_effects=True, vmem_limit_bytes=60 * 1024 * 1024
            ),
        )(tokens, cotangent, levels, gate_weight, up_weight, down_weight)
        return finish(mixed, grad, gate, up, down)

    return body


def solution(mesh):
    rows = P(("dp", "tensor"), None)
    columns = P(None, "tensor")
    units = P("tensor", None)
    return jax.shard_map(
        make_body(4, mesh.shape["tensor"] // 8, mesh.shape["dp"], 16384),
        mesh=mesh,
        in_specs=(rows, rows, P(), columns, columns, units),
        out_specs=(rows, rows, columns, columns, units),
        check_vma=False,
    )
```

time: 121 us -> 93.5 us (0.77)
  Pallas kernels: 114 us -> 92.7 us
  local copies, waits for them, and re-layouts: 6.51 us -> 0 us
    pallas_call x1, Pallas kernels: 114 us -> 89.4 us  [body(): pl.pallas_call(functools.partial(kernel, (nx, ny, nz, units, width, ff)),...]
    unnamed x11 -> x0, local copies, waits for them, and re-layouts: 4.79 us -> none
    pallas_call x0 -> x1, Pallas kernels: none -> 3.3 us  [finish(): pl.pallas_call(finish_kernel, out_shape=tuple((jax.ShapeDtypeStruct(s, BF...]
    transpose x1 -> x0, local copies, waits for them, and re-layouts: 1.73 us -> none  [body(): return (mixed, grad, gu[:units].T, gu[units:].T, down)]
where the time goes in v3:
time: 93.5 us; the launch traced here: 93.3 us
  Pallas kernels  92.7 us (99%)
    pallas_call x1, Pallas kernels, body(): pl.pallas_call(functools.partial(kernel, (nx, ny, nz, units, width, ff)),...  89.4 us
    pallas_call x1, Pallas kernels, finish(): pl.pallas_call(finish_kernel, out_shape=tuple((jax.ShapeDtypeStruct(s, BF...  3.3 us

profile of v3, /device:TPU:1, one launch (start us, length us, event | category | flops | bytes accessed | tf_op | source)
XLA Modules:
  0.0 93.3 jit_solution(5561698720652898563)
XLA Ops:
  0.6 89.4 %shard_map.101 = (bf16[2,2048]{1,0:T(2,128)(2,1)}, bf16[2,2048]{1,0:T(2,128)(2,1)}, bf16[256,2048]{1,0:T(8,128)(2,1)}, bf16[256,2048]{1,0:T(8,128)(2,1)}, bf16[256,2048]{1,0:T(8,128)(2,1)}) custom-call(bf16[2,2048]{1,0:T(2,128)(2,1)} %tok.1, bf16[2,2048]{1,0:T(2,128)(2,1)} %cot.1, s32[12]{0:T(128)} %lev.1, bf16[2048,256]{1,0:T(8,128)(2,1)} %gate_w.1, ...), custom_call_target="tpu_custom_call" | custom-call | tf_op jit(solution)/shard_map/pallas_call | solution.py:437
  90.0 3.3 %shard_map.102 = (bf16[2,2048]{1,0:T(2,128)(2,1)}, bf16[2,2048]{1,0:T(2,128)(2,1)}, bf16[2048,256]{1,0:T(8,128)(2,1)}, bf16[2048,256]{1,0:T(8,128)(2,1)}, bf16[256,2048]{1,0:T(8,128)(2,1)}) custom-call(bf16[2,2048]{1,0:T(2,128)(2,1)} %get-tuple-element.10.mixed, bf16[2,2048]{1,0:T(2,128)(2,1)} %get-tuple-element.11.grad, ...), custom_call_target="tpu_custom_call" | custom-call | tf_op jit(solution)/shard_map/pallas_call | solution.py:420

commit v4 on v3

--- a/solution.py
+++ b/solution.py
@@ -67,7 +67,6 @@
         acc[pl.ds(r * 8, 8), :] = jnp.zeros((8, width), F32)
         return carry
 
-    lax.fori_loop(0, 3 * units // 8, clear, 0)
     pl.semaphore_wait(barrier, greeted)
 
     def p0(src, landing, which, slot, sem_slot, target):
@@ -176,10 +175,6 @@
         col, zz, yy, target, last, m = p1_block(stream, 0)
         ring(col, zz, yy, target, p1_send.at[stream, 0]).start()
 
-    for copy in copies:
-        copy.wait()
-    dwt[...] = dw[...].T
-
     rows = ny * 16
 
     def groups_of(m):
@@ -230,18 +225,21 @@
         cols = slice(side * colour, (side + 1) * colour)
         first, second = groups_of(m)
         span = slice(down * width + side * colour, down * width + (side + 1) * colour)
-        value = jnp.concatenate(
-            [gath[first, :, :, span].reshape(rows, colour), gath[second, :, :, span].reshape(rows, colour)], axis=0
-        )
+
+        def rows_of():
+            return jnp.concatenate(
+                [gath[first, :, :, span].reshape(rows, colour), gath[second, :, :, span].reshape(rows, colour)], axis=0
+            )
+
         lines = slice(2 * units, 3 * units) if down else slice(0, 2 * units)
-        total = acc[lines, cols] + jnp.dot(act_t[lines, :], value, preferred_element_type=F32)
 
         @pl.when(m < chunks - 1)
         def _():
-            acc[lines, cols] = total
+            acc[lines, cols] += jnp.dot(act_t[lines, :], rows_of(), preferred_element_type=F32)
 
         @pl.when(m == chunks - 1)
         def _():
+            total = acc[lines, cols] + jnp.dot(act_t[lines, :], rows_of(), preferred_element_type=F32)
             if down:
                 down_out[:, cols] = total.astype(BF16)
             else:
@@ -347,9 +345,19 @@
             p1_step(t)
 
         def step(r, inner):
-            @pl.when(r <= hy)
+            @pl.when((r <= hy) & (t >= r) & (t - r <= hz))
             def _():
                 main_slot(t, r)
+
+            @pl.when((t == 1) & (r == hy + 1))
+            def _():
+                lax.fori_loop(0, 3 * units // 8, clear, 0)
+
+            @pl.when((t == 2) & (r == hy + 1))
+            def _():
+                for copy in copies:
+                    copy.wait()
+                dwt[...] = dw[...].T
 
             m = t - LEAD
             for q in range(PIECES):

time: 93.5 us -> 89.7 us (0.959)
  Pallas kernels: 92.7 us -> 88.9 us
    pallas_call x1, Pallas kernels: 89.4 us -> 85.6 us  [body(): pl.pallas_call(functools.partial(kernel, (nx, ny, nz, units, width, ff)),...]
where the time goes in v4:
time: 89.7 us; the launch traced here: 89.5 us
  Pallas kernels  88.9 us (99%)
    pallas_call x1, Pallas kernels, body(): pl.pallas_call(functools.partial(kernel, (nx, ny, nz, units, width, ff)),...  85.6 us
    pallas_call x1, Pallas kernels, finish(): pl.pallas_call(finish_kernel, out_shape=tuple((jax.ShapeDtypeStruct(s, BF...  3.3 us

profile of v4, /device:TPU:1, one launch (start us, length us, event | category | flops | bytes accessed | tf_op | source)
XLA Modules:
  0.0 89.5 jit_solution(12091957033438068390)
XLA Ops:
  0.6 85.6 %shard_map.101 = (bf16[2,2048]{1,0:T(2,128)(2,1)}, bf16[2,2048]{1,0:T(2,128)(2,1)}, bf16[256,2048]{1,0:T(8,128)(2,1)}, bf16[256,2048]{1,0:T(8,128)(2,1)}, bf16[256,2048]{1,0:T(8,128)(2,1)}) custom-call(bf16[2,2048]{1,0:T(2,128)(2,1)} %tok.1, bf16[2,2048]{1,0:T(2,128)(2,1)} %cot.1, s32[12]{0:T(128)} %lev.1, bf16[2048,256]{1,0:T(8,128)(2,1)} %gate_w.1, ...), custom_call_target="tpu_custom_call" | custom-call | tf_op jit(solution)/shard_map/pallas_call | solution.py:445
  86.2 3.3 %shard_map.102 = (bf16[2,2048]{1,0:T(2,128)(2,1)}, bf16[2,2048]{1,0:T(2,128)(2,1)}, bf16[2048,256]{1,0:T(8,128)(2,1)}, bf16[2048,256]{1,0:T(8,128)(2,1)}, bf16[256,2048]{1,0:T(8,128)(2,1)}) custom-call(bf16[2,2048]{1,0:T(2,128)(2,1)} %get-tuple-element.10.mixed, bf16[2,2048]{1,0:T(2,128)(2,1)} %get-tuple-element.11.grad, ...), custom_call_target="tpu_custom_call" | custom-call | tf_op jit(solution)/shard_map/pallas_call | solution.py:428
